TPU v7x, 32 devices: a whole 2x2x4 slice. The times are simulated.
32 devices in a mesh: grp: 8 (over y, x, core), blk: 4 (over z).
Axes of the slice: x: 2, y: 2, z: 4, core: 2. Of those that a mesh axis runs over, the one named last changes fastest.
Arguments:
- inputs: bfloat16 [8, 2, 1024, 640], P('grp', None, 'blk'), may hold values from -6 to 6
- cotangent: bfloat16 [8, 2, 1024, 640], P('grp', None, 'blk'), may hold values from -6 to 6
- master_attend: float32 [640, 1536], P('blk'), may hold values from -0.25 to 0.25
- master_merge: float32 [1024, 640], P('blk'), may hold values from -0.1875 to 0.1875
- master_expand: float32 [640, 4096], P('blk'), may hold values from -0.25 to 0.25
- master_reduce: float32 [2048, 640], P('blk'), may hold values from -0.125 to 0.125
- master_gains: float32 [3072], P('blk'), may hold values from -1 to 1
- moment_attend: float32 [640, 1536], P('blk'), may hold values from -3 to 3
- moment_merge: float32 [1024, 640], P('blk'), may hold values from -3 to 3
- moment_expand: float32 [640, 4096], P('blk'), may hold values from -3 to 3
- moment_reduce: float32 [2048, 640], P('blk'), may hold values from -3 to 3
- moment_gains: float32 [3072], P('blk'), may hold values from -3 to 3
- error_attend: float32 [8, 640, 1536], P('grp', 'blk'), may hold values from -192 to 192
- error_merge: float32 [8, 1024, 640], P('grp', 'blk'), may hold values from -192 to 192
- error_expand: float32 [8, 640, 4096], P('grp', 'blk'), may hold values from -192 to 192
- error_reduce: float32 [8, 2048, 640], P('grp', 'blk'), may hold values from -192 to 192
- start_attend: float32 [4, 1536, 8], P('blk'), may hold values from -6 to 6
- start_merge: float32 [4, 640, 8], P('blk'), may hold values from -6 to 6
- start_expand: float32 [4, 4096, 8], P('blk'), may hold values from -6 to 6
- start_reduce: float32 [4, 640, 8], P('blk'), may hold values from -6 to 6
Outputs:
- block_output: bfloat16 [8, 2, 1024, 640], P('grp', None, 'blk')
- input_grad: float32 [8, 2, 1024, 640], P('grp', None, 'blk')
- grad_attend: float32 [8, 640, 1536], P('grp', 'blk')
- grad_merge: float32 [8, 1024, 640], P('grp', 'blk')
- grad_expand: float32 [8, 640, 4096], P('grp', 'blk')
- grad_reduce: float32 [8, 2048, 640], P('grp', 'blk')
- grad_gains: float32 [8, 3072], P('grp', 'blk')
- left_attend: float32 [640, 8], P('blk')
- left_merge: float32 [1024, 8], P('blk')
- left_expand: float32 [640, 8], P('blk')
- left_reduce: float32 [2048, 8], P('blk')
- right_attend: float32 [4, 1536, 8], P('blk')
- right_merge: float32 [4, 640, 8], P('blk')
- right_expand: float32 [4, 4096, 8], P('blk')
- right_reduce: float32 [4, 640, 8], P('blk')
- residue_attend: float32 [8, 640, 1536], P('grp', 'blk')
- residue_merge: float32 [8, 1024, 640], P('grp', 'blk')
- residue_expand: float32 [8, 640, 4096], P('grp', 'blk')
- residue_reduce: float32 [8, 2048, 640], P('grp', 'blk')
- velocity_attend: float32 [640, 1536], P('blk')
- velocity_merge: float32 [1024, 640], P('blk')
- velocity_expand: float32 [640, 4096], P('blk')
- velocity_reduce: float32 [2048, 640], P('blk')
- velocity_gains: float32 [3072], P('blk')
- weight_attend: float32 [640, 1536], P('blk')
- weight_merge: float32 [1024, 640], P('blk')
- weight_expand: float32 [640, 4096], P('blk')
- weight_reduce: float32 [2048, 640], P('blk')
- weight_gains: float32 [3072], P('blk')
- copy_attend: bfloat16 [640, 1536], P('blk')
- copy_merge: bfloat16 [1024, 640], P('blk')
- copy_expand: bfloat16 [640, 4096], P('blk')
- copy_reduce: bfloat16 [2048, 640], P('blk')
- copy_gains: bfloat16 [3072], P('blk')
All inputs are finite; a program needn't handle non-finite values.
Results may differ from a plain program's by a relative error of at most 0.028.
Values may be sent and summed in bfloat16 or wider, within the bound.
No kernel may reach another device: no remote copies, remote signals or barrier semaphores. Data moves between devices by JAX's collectives and lax.ppermute only.
A program may use at most 192 MiB of HBM per device.

v0:
```python
import jax
import jax.numpy as jnp
from jax import lax
from jax.sharding import PartitionSpec as P

D = 640
NH = 4
HD = 256
FF = 2048
WINDOW = 512
SEG = 256
HQ = 1024
NORM_EPS = 1e-06
ROPE_BASE = 10000.0
ERROR_KEEP = 0.5
MOMENTUM = 0.9
STEP_RATE = 0.02
NEG_FILL = -1e30


def rmsnorm(values, gain_row):
    return (
        values
        * lax.rsqrt(jnp.mean(values * values, axis=-1, keepdims=True) + NORM_EPS)
        * (1.0 + gain_row)
    )


def rotate(values, cosine, sine_part):
    middle = values.shape[-1] // 2
    turned = jnp.concatenate([-values[..., middle:], values[..., :middle]], axis=-1)
    return values * cosine + turned * sine_part


def rope_tables(places):
    frequency = jnp.arange(HD // 2, dtype=jnp.float32)
    inverse = ROPE_BASE ** (-2.0 * frequency / HD)
    angles = places.astype(jnp.float32)[:, None] * inverse[None, :]
    angles = jnp.concatenate([angles, angles], axis=-1)
    return (jnp.cos(angles), jnp.sin(angles))


def prepare_heads(projected, gain_query, gain_key, cosine, sine_part):
    row_count = projected.shape[0]
    query_rows = projected[:, :HQ].reshape(row_count, NH, HD)
    keys_raw = projected[:, HQ : HQ + HD]
    values_raw = projected[:, HQ + HD :]
    query_rows = rotate(
        rmsnorm(query_rows, gain_query), cosine[:, None, :], sine_part[:, None, :]
    ) * HD ** (-0.5)
    keys_rot = rotate(rmsnorm(keys_raw, gain_key), cosine, sine_part)
    return (query_rows, keys_rot, values_raw)


def gated_gelu(gate_up):
    return jax.nn.gelu(gate_up[:, :FF], approximate=True) * gate_up[:, FF:]


def orthonormal(factor):
    columns = []
    for column in range(factor.shape[1]):
        vector = factor[:, column]
        for basis in columns:
            vector = vector - jnp.sum(basis * vector) * basis
        columns.append(vector * lax.rsqrt(jnp.sum(vector * vector) + NORM_EPS))
    return jnp.stack(columns, axis=1)


def contract_rows(left_side, right_side):
    return lax.dot_general(
        left_side, right_side, (((0,), (0,)), ((), ())), preferred_element_type=jnp.float32
    )


def contract_cols(left_side, right_side):
    return lax.dot_general(
        left_side, right_side, (((1,), (1,)), ((), ())), preferred_element_type=jnp.float32
    )


def on_device(
    inputs,
    cotangent,
    master_attend,
    master_merge,
    master_expand,
    master_reduce,
    master_gains,
    moment_attend,
    moment_merge,
    moment_expand,
    moment_reduce,
    moment_gains,
    error_attend,
    error_merge,
    error_expand,
    error_reduce,
    start_attend,
    start_merge,
    start_expand,
    start_reduce,
):
    blocks = lax.axis_size("blk")
    groups = lax.axis_size("grp")
    block_index = lax.axis_index("blk")
    prompt_size = SEG * blocks
    full_attend, full_merge, full_expand, full_reduce, gain_copy = (
        lax.all_gather(master_attend.astype(jnp.bfloat16), "blk", axis=0, tiled=True),
        lax.all_gather(master_merge.astype(jnp.bfloat16), "blk", axis=0, tiled=True),
        lax.all_gather(master_expand.astype(jnp.bfloat16), "blk", axis=0, tiled=True),
        lax.all_gather(master_reduce.astype(jnp.bfloat16), "blk", axis=0, tiled=True),
        lax.all_gather(master_gains.astype(jnp.bfloat16), "blk", axis=0, tiled=True),
    )
    gain_all = gain_copy.astype(jnp.float32)
    gain_first = gain_all[:D]
    gain_second = gain_all[D : 2 * D]
    gain_third = gain_all[2 * D : 3 * D]
    gain_fourth = gain_all[3 * D : 4 * D]
    gain_query = gain_all[4 * D : 4 * D + HD]
    gain_key = gain_all[4 * D + HD :]
    offsets = jnp.arange(SEG, dtype=jnp.int32)
    prompt_place = block_index * SEG + offsets
    reply_place = prompt_size + offsets
    cosine, sine_part = rope_tables(jnp.concatenate([prompt_place, reply_place]))
    rows_in = inputs[0].reshape(2 * SEG, D).astype(jnp.float32)
    normed_low = rmsnorm(rows_in, gain_first).astype(jnp.bfloat16)
    projected = jnp.dot(normed_low, full_attend, preferred_element_type=jnp.float32)
    query_rows, keys_rot, values_raw = prepare_heads(
        projected, gain_query, gain_key, cosine, sine_part
    )
    query_reduced = query_rows.astype(jnp.bfloat16).reshape(2, SEG, NH, HD)
    pair_low = jnp.concatenate([keys_rot, values_raw], axis=-1).astype(jnp.bfloat16)
    prompt_pairs = lax.all_gather(pair_low[:SEG], "blk", axis=0, tiled=True)
    padded = jnp.concatenate([jnp.zeros((WINDOW, 2 * HD), jnp.bfloat16), prompt_pairs], axis=0)
    window_pairs = lax.dynamic_slice_in_dim(padded, block_index * SEG, WINDOW + SEG, 0)
    reply_pairs = jnp.concatenate([prompt_pairs[prompt_size - WINDOW :], pair_low[SEG:]], axis=0)
    key_sets = jnp.stack([window_pairs, reply_pairs])
    key_reduced = key_sets[..., :HD]
    value_reduced = key_sets[..., HD:]
    span = jnp.arange(WINDOW + SEG, dtype=jnp.int32)
    key_place = jnp.stack(
        [
            block_index * SEG - WINDOW + span,
            jnp.where(span < WINDOW, prompt_size - WINDOW + span, prompt_size + span - WINDOW),
        ]
    )
    query_place = jnp.stack([prompt_place, reply_place])
    distance = query_place[:, :, None] - key_place[:, None, :]
    allowed = (key_place[:, None, :] >= 0) & (distance >= 0) & (distance < WINDOW)

    def score_block():
        products = jnp.einsum(
            "itge,iue->igtu", query_reduced, key_reduced, preferred_element_type=jnp.float32
        )
        return jnp.where(allowed[:, None], products, NEG_FILL)

    attention_scores = score_block()
    top_score = jnp.max(attention_scores, axis=-1, keepdims=True)
    log_total = top_score + jnp.log(
        jnp.sum(jnp.exp(attention_scores - top_score), axis=-1, keepdims=True)
    )
    probability_reduced = jnp.exp(attention_scores - log_total).astype(jnp.bfloat16)
    attended = jnp.einsum(
        "ayco,aox->acyx", probability_reduced, value_reduced, preferred_element_type=jnp.float32
    )
    attended_low = attended.reshape(2 * SEG, HQ).astype(jnp.bfloat16)
    branch_attn = jnp.dot(attended_low, full_merge, preferred_element_type=jnp.float32)
    hidden = rows_in + rmsnorm(branch_attn, gain_second)
    normed_mid = rmsnorm(hidden, gain_third).astype(jnp.bfloat16)
    gate_up = jnp.dot(normed_mid, full_expand, preferred_element_type=jnp.float32)
    activated = gated_gelu(gate_up).astype(jnp.bfloat16)
    branch_ff = jnp.dot(activated, full_reduce, preferred_element_type=jnp.float32)
    result = hidden + rmsnorm(branch_ff, gain_fourth)
    block_output = result.astype(jnp.bfloat16).reshape(1, 2, SEG, D)
    upstream = cotangent[0].reshape(2 * SEG, D).astype(jnp.float32)
    _, outer_back = jax.vjp(rmsnorm, branch_ff, gain_fourth)
    branch_grad, grad_fourth = outer_back(upstream)
    branch_low = branch_grad.astype(jnp.bfloat16)
    grad_reduce = contract_rows(activated, branch_low)
    active_grad = contract_cols(branch_low, full_reduce)
    _, gelu_back = jax.vjp(gated_gelu, gate_up)
    (expand_grad,) = gelu_back(active_grad)
    expand_low = expand_grad.astype(jnp.bfloat16)
    grad_expand = contract_rows(normed_mid, expand_low)
    middle_grad = contract_cols(expand_low, full_expand)
    _, third_back = jax.vjp(rmsnorm, hidden, gain_third)
    hidden_part, grad_third = third_back(middle_grad)
    hidden_grad = upstream + hidden_part
    _, second_back = jax.vjp(rmsnorm, branch_attn, gain_second)
    attn_grad, grad_second = second_back(hidden_grad)
    attn_low = attn_grad.astype(jnp.bfloat16)
    grad_merge = contract_rows(attended_low, attn_low)
    context_reduced = (
        contract_cols(attn_low, full_merge).astype(jnp.bfloat16).reshape(2, SEG, NH, HD)
    )
    attention_probabilities = jnp.exp(score_block() - log_total)
    probability_recomputed = attention_probabilities.astype(jnp.bfloat16)
    value_grad = jnp.einsum(
        "jsze,jzsf->jef",
        probability_recomputed,
        context_reduced,
        preferred_element_type=jnp.float32,
    )
    chance_grad = jnp.einsum(
        "itge,iue->igtu", context_reduced, value_reduced, preferred_element_type=jnp.float32
    )
    inner_sum = jnp.sum(attention_probabilities * chance_grad, axis=-1, keepdims=True)
    score_reduced = (attention_probabilities * (chance_grad - inner_sum)).astype(jnp.bfloat16)
    query_grad = jnp.einsum(
        "ayco,aox->acyx", score_reduced, key_reduced, preferred_element_type=jnp.float32
    )
    key_grad = jnp.einsum(
        "jsze,jzsf->jef", score_reduced, query_reduced, preferred_element_type=jnp.float32
    )
    pair_grad = jnp.concatenate([key_grad, value_grad], axis=-1)
    spread = jnp.zeros((WINDOW + prompt_size, 2 * HD), jnp.float32)
    spread = lax.dynamic_update_slice_in_dim(spread, pair_grad[0], block_index * SEG, 0)
    spread = jnp.concatenate(
        [spread[:prompt_size], spread[prompt_size:] + pair_grad[1, :WINDOW]], axis=0
    )
    owned_pairs = lax.psum_scatter(
        spread[WINDOW:].astype(jnp.bfloat16), "blk", scatter_dimension=0, tiled=True
    ).astype(jnp.float32)
    pair_rows = jnp.concatenate([owned_pairs, pair_grad[1, WINDOW:]], axis=0)

    def head_section(mixed_rows, query_gain, key_gain):
        return prepare_heads(mixed_rows, query_gain, key_gain, cosine, sine_part)

    _, heads_back = jax.vjp(head_section, projected, gain_query, gain_key)
    mixed_grad, grad_query, grad_key = heads_back(
        (query_grad.reshape(2 * SEG, NH, HD), pair_rows[:, :HD], pair_rows[:, HD:])
    )
    mixed_low = mixed_grad.astype(jnp.bfloat16)
    grad_attend = contract_rows(normed_low, mixed_low)
    normed_grad = contract_cols(mixed_low, full_attend)
    _, first_back = jax.vjp(rmsnorm, rows_in, gain_first)
    input_part, grad_first = first_back(normed_grad)
    input_grad = (hidden_grad + input_part).reshape(1, 2, SEG, D)
    gain_grads = jnp.concatenate(
        [grad_first, grad_second, grad_third, grad_fourth, grad_query, grad_key]
    )
    owned_attend, owned_merge, owned_expand, owned_reduce, owned_gains = (
        lax.psum_scatter(
            grad_attend.astype(jnp.bfloat16), "blk", scatter_dimension=0, tiled=True
        ).astype(jnp.float32),
        lax.psum_scatter(
            grad_merge.astype(jnp.bfloat16), "blk", scatter_dimension=0, tiled=True
        ).astype(jnp.float32),
        lax.psum_scatter(
            grad_expand.astype(jnp.bfloat16), "blk", scatter_dimension=0, tiled=True
        ).astype(jnp.float32),
        lax.psum_scatter(
            grad_reduce.astype(jnp.bfloat16), "blk", scatter_dimension=0, tiled=True
        ).astype(jnp.float32),
        lax.psum_scatter(
            gain_grads.astype(jnp.bfloat16), "blk", scatter_dimension=0, tiled=True
        ).astype(jnp.float32),
    )
    owned_all = (owned_attend, owned_merge, owned_expand, owned_reduce)
    buffers = (error_attend, error_merge, error_expand, error_reduce)
    factors = (start_attend, start_merge, start_expand, start_reduce)
    combined = [owned + ERROR_KEEP * buffer[0] for owned, buffer in zip(owned_all, buffers)]
    lefts = [
        jnp.dot(matrix, factor[0], precision=lax.Precision.HIGHEST)
        for matrix, factor in zip(combined, factors)
    ]
    left_sums = lax.psum((lefts[0], lefts[1], lefts[2], lefts[3], owned_gains), "grp")
    basis_set = [orthonormal(left_sums[member]) for member in range(4)]
    rights = [
        lax.dot_general(matrix, basis, (((0,), (0,)), ((), ())), precision=lax.Precision.HIGHEST)
        for matrix, basis in zip(combined, basis_set)
    ]
    right_sums = (
        lax.psum(rights[0].astype(jnp.bfloat16), "grp").astype(jnp.float32),
        lax.psum(rights[1].astype(jnp.bfloat16), "grp").astype(jnp.float32),
        lax.psum(rights[2].astype(jnp.bfloat16), "grp").astype(jnp.float32),
        lax.psum(rights[3].astype(jnp.bfloat16), "grp").astype(jnp.float32),
    )
    residues = [
        matrix - jnp.dot(basis, partial_right.T, precision=lax.Precision.HIGHEST)
        for matrix, basis, partial_right in zip(combined, basis_set, rights)
    ]
    directions = [
        jnp.dot(basis, summed.T, precision=lax.Precision.HIGHEST) / groups
        for basis, summed in zip(basis_set, right_sums)
    ]
    directions.append(left_sums[4] / groups)
    moments = (moment_attend, moment_merge, moment_expand, moment_reduce, moment_gains)
    masters = (master_attend, master_merge, master_expand, master_reduce, master_gains)
    velocities = [
        MOMENTUM * moment + (1.0 - MOMENTUM) * direction
        for moment, direction in zip(moments, directions)
    ]
    updated = [master - STEP_RATE * velocity for master, velocity in zip(masters, velocities)]
    return (
        block_output,
        input_grad,
        owned_attend[None],
        owned_merge[None],
        owned_expand[None],
        owned_reduce[None],
        owned_gains[None],
        basis_set[0],
        basis_set[1],
        basis_set[2],
        basis_set[3],
        right_sums[0][None],
        right_sums[1][None],
        right_sums[2][None],
        right_sums[3][None],
        residues[0][None],
        residues[1][None],
        residues[2][None],
        residues[3][None],
        velocities[0],
        velocities[1],
        velocities[2],
        velocities[3],
        velocities[4],
        updated[0],
        updated[1],
        updated[2],
        updated[3],
        updated[4],
        updated[0].astype(jnp.bfloat16),
        updated[1].astype(jnp.bfloat16),
        updated[2].astype(jnp.bfloat16),
        updated[3].astype(jnp.bfloat16),
        updated[4].astype(jnp.bfloat16),
    )


def solution(mesh):
    in_specs = (
        P("grp", None, "blk", None),
        P("grp", None, "blk", None),
        P("blk", None),
        P("blk", None),
        P("blk", None),
        P("blk", None),
        P("blk"),
        P("blk", None),
        P("blk", None),
        P("blk", None),
        P("blk", None),
        P("blk"),
        P("grp", "blk", None),
        P("grp", "blk", None),
        P("grp", "blk", None),
        P("grp", "blk", None),
        P("blk", None, None),
        P("blk", None, None),
        P("blk", None, None),
        P("blk", None, None),
    )
    out_specs = (
        P("grp", None, "blk", None),
        P("grp", None, "blk", None),
        P("grp", "blk", None),
        P("grp", "blk", None),
        P("grp", "blk", None),
        P("grp", "blk", None),
        P("grp", "blk"),
        P("blk", None),
        P("blk", None),
        P("blk", None),
        P("blk", None),
        P("blk", None, None),
        P("blk", None, None),
        P("blk", None, None),
        P("blk", None, None),
        P("grp", "blk", None),
        P("grp", "blk", None),
        P("grp", "blk", None),
        P("grp", "blk", None),
        P("blk", None),
        P("blk", None),
        P("blk", None),
        P("blk", None),
        P("blk"),
        P("blk", None),
        P("blk", None),
        P("blk", None),
        P("blk", None),
        P("blk"),
        P("blk", None),
        P("blk", None),
        P("blk", None),
        P("blk", None),
        P("blk"),
    )
    return jax.shard_map(
        on_device, mesh=mesh, in_specs=in_specs, out_specs=out_specs, check_vma=False
    )
```

profile of v0, /device:TPU:0, one launch (start us, length us, event | category | flops | bytes accessed | tf_op | source)
XLA Modules:
  0.0 946.2 jit_solution(14591315327089073494)
XLA Ops:
  10.2 14.9 %all-gather = bf16[4,1,768]{2,1,0:T(2,128)(2,1)S(1)} all-gather(bf16[1,1,768]{2,1,0:T(2,128)(2,1)S(1)} %reshape.422), channel_id=1, replica_groups=mesh['grp'=8,'blk'=4] {'blk'}, dimensions={0}, use_global_device_ids=true | all-gather | bytes 7680 | tf_op jit(solution)/shard_map/all_gather | solution.py:112
  27.0 29.5 %all-gather.7.cloned.1.call-done = bf16[640,1536]{1,0:T(8,128)(2,1)} async-done(((bf16[160,1536]{1,0:T(8,128)(2,1)}), bf16[640,1536]{1,0:T(8,128)(2,1)}) %all-gather.7.cloned.1.call-update) | async-done | bytes 1966096 | tf_op jit(solution)/shard_map/all_gather | solution.py:108
  56.5 2.9 fusion.142
  69.1 2.8 fusion.83
  83.9 6.4 all-gather.9.cloned.1.call-done
  98.5 25.9 %all-gather.11.cloned.1.call-done = bf16[1024,640]{1,0:T(8,128)(2,1)} async-done(((bf16[256,640]{1,0:T(8,128)(2,1)}), bf16[1024,640]{1,0:T(8,128)(2,1)}) %all-gather.11.cloned.1.call-update) | async-done | bytes 1310736 | tf_op jit(solution)/shard_map/all_gather | solution.py:109
  127.8 95.7 %all-gather.13.cloned.1.call-done = bf16[640,4096]{1,0:T(8,128)(2,1)} async-done(((bf16[160,4096]{1,0:T(8,128)(2,1)}), bf16[640,4096]{1,0:T(8,128)(2,1)}) %all-gather.13.cloned.1.call-update) | async-done | bytes 5242896 | tf_op jit(solution)/shard_map/all_gather | solution.py:110
  223.5 5.5 fusion.123
  229.0 3.3 copy-done.4
  232.4 2.6 multiply_convert_fusion
  235.0 43.6 %all-gather.15.cloned.1.call-done = bf16[2048,640]{1,0:T(8,128)(2,1)} async-done(((bf16[512,640]{1,0:T(8,128)(2,1)}), bf16[2048,640]{1,0:T(8,128)(2,1)}) %all-gather.15.cloned.1.call-update) | async-done | bytes 2621456 | tf_op jit(solution)/shard_map/all_gather | solution.py:111
  278.6 4.4 multiply_reduce_fusion.6
  285.5 4.9 fusion.34
  290.6 4.1 multiply_reduce_fusion.2
  300.5 2.9 copy.142
  303.5 5.3 fusion
  310.3 3.2 fusion.2
  313.5 3.1 convolution_bitcast_fusion.2
  319.3 3.6 convolution_convert_fusion.3
  323.0 4.4 convolution_convert_fusion.1
  328.8 3.2 convolution_bitcast_fusion
  334.8 10.6 %reduce-scatter.6.cloned.1.call-done = bf16[256,512]{1,0:T(8,128)(2,1)} async-done(((bf16[1024,512]{1,0:T(8,128)(2,1)}), bf16[256,512]{1,0:T(8,128)(2,1)}) %reduce-scatter.6.cloned.1.call-update) | async-done | bytes 262160 | tf_op jit(solution)/shard_map/reduce_scatter | solution.py:221
  346.5 3.0 fusion.76
  349.7 3.6 multiply_reduce_fusion.9
  363.3 8.8 convolution_convert_fusion
  374.2 4.8 fusion.46
  380.2 9.7 %all-reduce.10 = bf16[3072]{0:T(1024)(128)(2,1)S(1)} all-reduce(bf16[3072]{0:T(1024)(128)(2,1)S(1)} %dynamic-update-slice.5), channel_id=7, replica_groups=mesh['grp'=8,'blk'=4] {'blk'}, use_global_device_ids=true, to_apply=%region_26.27.clone | all-reduce | flops 3072 | bytes 12288
  390.6 2.8 fusion.41
  396.9 35.1 %reduce-scatter.14.cloned.1.call-done = bf16[512,640]{1,0:T(8,128)(2,1)} async-done(((bf16[2048,640]{1,0:T(8,128)(2,1)}), bf16[512,640]{1,0:T(8,128)(2,1)}) %reduce-scatter.14.cloned.1.call-update) | async-done | bytes 655376 | tf_op jit(solution)/shard_map/reduce_scatter | solution.py:252
  434.3 2.8 fusion.85
  437.1 39.0 %reduce-scatter.8.cloned.1.call-done = bf16[160,1536]{1,0:T(8,128)(2,1)} async-done(((bf16[640,1536]{1,0:T(8,128)(2,1)}), bf16[160,1536]{1,0:T(8,128)(2,1)}) %reduce-scatter.8.cloned.1.call-update) | async-done | bytes 491536 | tf_op jit(solution)/shard_map/reduce_scatter | solution.py:243
  480.5 90.7 %reduce-scatter.12.cloned.1.call-done = bf16[160,4096]{1,0:T(8,128)(2,1)} async-done(((bf16[640,4096]{1,0:T(8,128)(2,1)}), bf16[160,4096]{1,0:T(8,128)(2,1)}) %reduce-scatter.12.cloned.1.call-update) | async-done | bytes 1310736 | tf_op jit(solution)/shard_map/reduce_scatter | solution.py:249
  571.2 3.5 fusion.66
  574.7 25.0 %all-reduce.11 = (f32[160,8]{0,1:T(8,128)S(1)}, f32[256,8]{0,1:T(8,128)S(1)}, f32[160,8]{0,1:T(8,128)S(1)}, f32[512,8]{0,1:T(8,128)S(1)}, f32[768]{0:T(1024)}) all-reduce(f32[160,8]{0,1:T(8,128)S(1)} %fusion.88, f32[256,8]{0,1:T(8,128)S(1)} %fusion.92, f32[160,8]{0,1:T(8,128)S(1)} %fusion.66, ...), channel_id=1, replica_groups=mesh['grp'=8,'blk'=4] {'grp'}, use_global_device_ids=true, to_apply=%region_27.28 | all-reduce | flops 9472 | bytes 75776 | tf_op jit(solution)/shard_map/psum | solution.py:267
  603.6 5.1 multiply_reduce_fusion.126
  613.2 6.4 multiply_reduce_fusion.125
  620.3 3.8 multiply_reduce_fusion.124
  628.7 3.8 multiply_reduce_fusion.123
  633.2 2.5 multiply_reduce_fusion.122
  642.2 18.1 %subtract_multiply_fusion.21 = (f32[160,1]{0,1:T(1,128)S(1)}, f32[160,1]{0,1:T(1,128)S(1)}, f32[160,1]{0,1:T(1,128)S(1)}, f32[160,1]{0,1:T(1,128)S(1)}, f32[160,...) fusion(f32[160,1]{0,1:T(1,128)S(1)} %get-tuple-element.344, f32[]{:T(128)S(6)} %rsqrt.180, ...), kind=kLoop, calls=%fused_computation.453 | loop fusion | flops 10080 | bytes 9740 | tf_op jit(solution)/shard_map/mul | solution.py:65
  664.2 5.1 multiply_reduce_fusion.90
  673.9 6.4 multiply_reduce_fusion.89
  681.0 3.8 multiply_reduce_fusion.88
  689.3 3.8 multiply_reduce_fusion.87
  693.9 2.5 multiply_reduce_fusion.86
  702.9 18.1 %subtract_multiply_fusion.14 = (f32[256,1]{0,1:T(1,128)S(1)}, f32[256,1]{0,1:T(1,128)S(1)}, f32[256,1]{0,1:T(1,128)S(1)}, f32[256,1]{0,1:T(1,128)S(1)}, f32[256,...) fusion(f32[256,1]{0,1:T(1,128)S(1)} %get-tuple-element.336, f32[]{:T(128)S(6)} %rsqrt.188, ...), kind=kLoop, calls=%fused_computation.383 | loop fusion | flops 16128 | bytes 15500 | tf_op jit(solution)/shard_map/mul | solution.py:65
  724.9 5.1 multiply_reduce_fusion.54
  734.5 6.4 multiply_reduce_fusion.53
  741.7 3.9 multiply_reduce_fusion.52
  750.0 3.8 multiply_reduce_fusion.51
  763.4 18.5 %subtract_multiply_fusion.7 = (f32[160,1]{0,1:T(1,128)}, f32[160,1]{0,1:T(1,128)}, f32[160,1]{0,1:T(1,128)}, f32[160,1]{0,1:T(1,128)}, f32[160,1]{0,1:T(1,128)}, /*index=5*/f32[160,1]{0,1:T(1,128)}, f32[160,1]{0,1:T(1,128)}) fusion(f32[160,1]{0,1:T(1,128)S(1)} %get-tuple-element.328, f32[]{:T(128)S(6)} %rsqrt.196, f32[]{:T(128)} %get-tuple-element.208, ...), kind=kLoop, calls=%fused_computation.313 | loop fusion | flops 10080 | bytes 9740 | tf_op jit(solution)/shard_map/mul | solution.py:65
  785.8 5.1 multiply_reduce_fusion.18
  795.4 6.4 multiply_reduce_fusion.17
  802.5 3.9 multiply_reduce_fusion.16
  810.8 3.8 multiply_reduce_fusion.15
  825.5 18.0 %subtract_multiply_fusion = (f32[512,1]{0,1:T(1,128)S(1)}, f32[512,1]{0,1:T(1,128)S(1)}, f32[512,1]{0,1:T(1,128)S(1)}, f32[512,1]{0,1:T(1,128)S(1)}, f32[512,1]{...) fusion(f32[512,1]{0,1:T(1,128)S(1)} %get-tuple-element.314, f32[]{:T(128)S(6)} %rsqrt.204, ...), kind=kLoop, calls=%fused_computation.222 | loop fusion | flops 32256 | bytes 30860 | tf_op jit(solution)/shard_map/mul | solution.py:65
  843.7 2.8 fusion.138
  850.3 23.6 %all-reduce.12 = (bf16[1536,8]{0,1:T(8,128)(2,1)S(1)}, bf16[640,8]{0,1:T(8,128)(2,1)S(1)}, bf16[640,8]{0,1:T(8,128)(2,1)}) all-reduce(bf16[1536,8]{0,1:T(8,128)(2,1)S(1)} %get-tuple-element.361, bf16[640,8]{0,1:T(8,128)(2,1)S(1)} %get-tuple-element.363, ...), channel_id=1, replica_groups=mesh['grp'=8,'blk'=4] {'grp'}, use_global_device_ids=true, to_apply=%region_175.176 | all-reduce | flops 22528 | bytes 90112 | tf_op jit(solution)/shard_map/psum | solution.py:274
  875.9 3.6 fusion.141
  880.9 3.8 fusion.129
  886.8 2.7 fusion.126
  894.0 4.0 fusion.4
  902.0 29.5 %all-reduce.15.cloned.1.call-done = bf16[4096,8]{0,1:T(8,128)(2,1)} async-done(((bf16[4096,8]{0,1:T(8,128)(2,1)}), bf16[4096,8]{0,1:T(8,128)(2,1)}) %all-reduce.15.cloned.1.call-update) | async-done | bytes 65552 | tf_op jit(solution)/shard_map/psum | solution.py:276
  933.1 6.3 fusion.127
  (439 shorter events, 164.2 us)
Async XLA Ops:
  7.2 564.0 %copy-start = (f32[1,4096,8]{1,2,0:T(8,128)S(1)}, f32[1,4096,8]{1,2,0:T(8,128)}, u32[]{:S(2)}) copy-start(f32[1,4096,8]{1,2,0:T(8,128)} %param.38) | copy-start | bytes 393220
  7.2 17.9 %copy-start.22 = (bf16[1,2,256,640]{3,2,1,0:T(8,128)(2,1)S(1)}, bf16[1,2,256,640]{3,2,1,0:T(8,128)(2,1)}, u32[]{:S(2)}) copy-start(bf16[1,2,256,640]{3,2,1,0:T(8,128)(2,1)} %param.20) | copy-start | bytes 1966084
  7.2 49.2 %all-gather.7.cloned.1.call-start = ((), (), s32[]{:S(2)}) async-start(), calls=%async_computation.5 | async-start | bytes 2457600 | tf_op jit(solution)/shard_map/all_gather | solution.py:108
  9.4 80.9 %all-gather.9.cloned.1.call-start = ((), (), s32[]{:S(2)}) async-start(), calls=%async_computation.6 | async-start | bytes 1310720 | tf_op jit(solution)/shard_map/all_gather | solution.py:133
  25.4 31.1 %copy-start.94 = (f32[512]{0:T(512)}, f32[512]{0:T(512)S(1)}, u32[]{:S(2)}) copy-start(f32[512]{0:T(512)S(1)} %rsqrt.166) | copy-start | bytes 6148
  25.4 31.1 %copy-start.114 = (f32[128]{0:T(128)}, f32[128]{0:T(128)S(1)}, u32[]{:S(2)}) copy-start(f32[128]{0:T(128)S(1)} %multiply_power_fusion) | copy-start | bytes 1540
  26.0 34.4 %copy-start.88 = (f32[256]{0:T(256)}, f32[256]{0:T(256)S(1)}, u32[]{:S(2)}) copy-start(f32[256]{0:T(256)S(1)} %get-tuple-element.325) | copy-start | bytes 3076
  26.6 29.9 %copy-start.85 = (f32[640]{0:T(1024)}, f32[640]{0:T(1024)S(1)}, u32[]{:S(2)}) copy-start(f32[640]{0:T(1024)S(1)} %get-tuple-element.324) | copy-start | bytes 7684
  26.6 100.8 %copy-start.77 = (f32[640]{0:T(1024)}, f32[640]{0:T(1024)S(1)}, u32[]{:S(2)}) copy-start(f32[640]{0:T(1024)S(1)} %get-tuple-element.323) | copy-start | bytes 7684
  26.7 33.6 %copy-start.42 = (f32[512,128]{1,0:T(8,128)}, f32[512,128]{1,0:T(8,128)S(1)}, u32[]{:S(2)}) copy-start(f32[512,128]{1,0:T(8,128)S(1)} %broadcast_multiply_fusion.1) | copy-start | bytes 786436
  27.0 32.4 %copy-start.55 = (bf16[512,640]{1,0:T(8,128)(2,1)}, bf16[512,640]{1,0:T(8,128)(2,1)S(1)}, u32[]{:S(2)}) copy-start(bf16[512,640]{1,0:T(8,128)(2,1)S(1)} %fusion.45) | copy-start | bytes 1966084
  59.9 5.5 copy-start.20
  63.3 61.0 %all-gather.11.cloned.1.call-start = ((), (), s32[]{:S(2)}) async-start(), calls=%async_computation.7 | async-start | bytes 1638400 | tf_op jit(solution)/shard_map/all_gather | solution.py:109
  65.3 158.3 %all-gather.13.cloned.1.call-start = ((), (), s32[]{:S(2)}) async-start(), calls=%async_computation.8 | async-start | bytes 6553600 | tf_op jit(solution)/shard_map/all_gather | solution.py:110
  66.6 212.1 %all-gather.15.cloned.1.call-start = ((), (), s32[]{:S(2)}) async-start(), calls=%async_computation.9 | async-start | bytes 3276800 | tf_op jit(solution)/shard_map/all_gather | solution.py:111
  68.8 276.7 %reduce-scatter.6.cloned.1.call-start = ((), (), s32[]{:S(2)}) async-start(), calls=%async_computation.10 | async-start | bytes 1310720 | tf_op jit(solution)/shard_map/reduce_scatter | solution.py:221
  72.6 21.8 %copy-start.26 = (pred[2,256,768]{1,2,0:T(8,128)(4,1)}, pred[2,256,768]{1,2,0:T(8,128)(4,1)S(1)}, u32[]{:S(2)}) copy-start(pred[2,256,768]{1,2,0:T(8,128)(4,1)S(1)} %fusion.31) | copy-start | bytes 1179652
  74.4 6.4 copy-start.2
  83.9 8.1 copy-start.44
  98.5 28.3 %copy-start.52 = (bf16[64,8,4,256]{3,1,2,0:T(8,128)(2,1)}, bf16[64,8,4,256]{3,1,2,0:T(8,128)(2,1)S(1)}, u32[]{:S(2)}) copy-start(bf16[64,8,4,256]{3,1,2,0:T(8,128)(2,1)S(1)} %copy.168) | copy-start | bytes 3145732
  235.0 48.0 %copy-start.34 = (bf16[1,2,256,640]{3,2,1,0:T(8,128)(2,1)S(1)}, bf16[1,2,256,640]{3,2,1,0:T(8,128)(2,1)}, u32[]{:S(2)}) copy-start(bf16[1,2,256,640]{3,2,1,0:T(8,128)(2,1)} %param.21) | copy-start | bytes 1966084
  235.0 48.0 %copy-start.87 = (f32[640]{0:T(1024)S(1)}, f32[640]{0:T(1024)}, u32[]{:S(2)}) copy-start(f32[640]{0:T(1024)} %get-tuple-element.321) | copy-start | bytes 7684
  278.6 6.9 copy-start.5
  284.2 6.4 slice-start.2
  285.5 5.0 copy-start.54
  285.5 5.0 slice-start.3
  300.5 8.3 slice-start
  303.4 5.3 slice-start.1
  303.4 5.3 copy-start.27
  303.4 5.3 copy-start.41
  303.5 5.3 copy-start.74
  310.3 7.0 copy-start.8
  319.2 74.2 %reduce-scatter.10.cloned.1.call-start = ((), (), s32[]{:S(2)}) async-start(), calls=%async_computation.12 | async-start | bytes 1638400 | tf_op jit(solution)/shard_map/reduce_scatter | solution.py:246
  322.9 109.1 %reduce-scatter.14.cloned.1.call-start = ((), (), s32[]{:S(2)}) async-start(), calls=%async_computation.14 | async-start | bytes 3276800 | tf_op jit(solution)/shard_map/reduce_scatter | solution.py:252
  327.5 148.7 %reduce-scatter.8.cloned.1.call-start = ((), (), s32[]{:S(2)}) async-start(), calls=%async_computation.11 | async-start | bytes 2457600 | tf_op jit(solution)/shard_map/reduce_scatter | solution.py:243
  345.5 4.2 copy-start.89
  353.3 6.6 copy-start.58
  363.2 208.0 %reduce-scatter.12.cloned.1.call-start = ((), (), s32[]{:S(2)}) async-start(), calls=%async_computation.13 | async-start | bytes 6553600 | tf_op jit(solution)/shard_map/reduce_scatter | solution.py:249
  372.2 559.3 %all-reduce.15.cloned.1.call-start = ((), (), s32[]{:S(2)}) async-start(), calls=%async_computation.15 | async-start | bytes 131072 | tf_op jit(solution)/shard_map/psum | solution.py:276
  374.1 5.1 copy-start.102
  374.1 5.3 copy-start.118
  374.1 5.5 copy-start.101
  374.1 5.7 copy-start.117
  374.1 5.9 copy-start.116
  374.1 16.5 %copy-start.99 = (f32[1,2,2,128]{3,1,2,0:T(2,128)S(1)}, f32[1,2,2,128]{3,1,2,0:T(2,128)}, u32[]{:S(2)}) copy-start(f32[1,2,2,128]{3,1,2,0:T(2,128)} %copy-done.98) | copy-start | bytes 6148
  374.1 16.5 %copy-start.19 = (f32[512,640]{1,0:T(8,128)S(1)}, f32[512,640]{1,0:T(8,128)}, u32[]{:S(2)}) copy-start(f32[512,640]{1,0:T(8,128)} %copy-done.18) | copy-start | bytes 3932164
  390.6 4.7 copy-start.32
  390.6 4.7 copy-start.93
  393.4 40.9 %copy-start.92 = (f32[1,640,8]{1,2,0:T(8,128)S(1)}, f32[1,640,8]{1,2,0:T(8,128)}, u32[]{:S(2)}) copy-start(f32[1,640,8]{1,2,0:T(8,128)} %param.39) | copy-start | bytes 61444
  396.9 79.2 %copy-start.81 = (f32[1,1536,8]{1,2,0:T(8,128)S(1)}, f32[1,1536,8]{1,2,0:T(8,128)}, u32[]{:S(2)}) copy-start(f32[1,1536,8]{1,2,0:T(8,128)} %param.36) | copy-start | bytes 147460
  434.3 136.9 %copy-start.6 = (f32[1,160,4096]{2,1,0:T(8,128)S(1)}, f32[1,160,4096]{2,1,0:T(8,128)}, u32[]{:S(2)}) copy-start(f32[1,160,4096]{2,1,0:T(8,128)} %param.34) | copy-start | bytes 7864324
  843.5 6.8 copy-start.64
  843.6 6.8 copy-start.66
  843.6 54.4 %copy-start.62 = (f32[512,8]{0,1:T(8,128)}, f32[512,8]{0,1:T(8,128)S(1)}, u32[]{:S(2)}) copy-start(f32[512,8]{0,1:T(8,128)S(1)} %stack.26) | copy-start | bytes 49156
  843.6 5.2 copy-start.16
  843.6 31.6 %copy-start.105 = (f32[160,1]{0,1:T(1,128)S(1)}, f32[160,1]{0,1:T(1,128)}, u32[]{:S(2)}) copy-start(f32[160,1]{0,1:T(1,128)} %get-tuple-element.201) | copy-start | bytes 1924
  843.6 31.6 %copy-start.106 = (f32[160,1]{0,1:T(1,128)S(1)}, f32[160,1]{0,1:T(1,128)}, u32[]{:S(2)}) copy-start(f32[160,1]{0,1:T(1,128)} %get-tuple-element.202) | copy-start | bytes 1924
  843.7 31.6 %copy-start.107 = (f32[160,1]{0,1:T(1,128)S(1)}, f32[160,1]{0,1:T(1,128)}, u32[]{:S(2)}) copy-start(f32[160,1]{0,1:T(1,128)} %get-tuple-element.203) | copy-start | bytes 1924
  843.7 31.5 %copy-start.108 = (f32[160,1]{0,1:T(1,128)S(1)}, f32[160,1]{0,1:T(1,128)}, u32[]{:S(2)}) copy-start(f32[160,1]{0,1:T(1,128)} %get-tuple-element.204) | copy-start | bytes 1924
  843.7 31.5 %copy-start.109 = (f32[160,1]{0,1:T(1,128)S(1)}, f32[160,1]{0,1:T(1,128)}, u32[]{:S(2)}) copy-start(f32[160,1]{0,1:T(1,128)} %get-tuple-element.205) | copy-start | bytes 1924
  843.7 31.5 %copy-start.110 = (f32[160,1]{0,1:T(1,128)S(1)}, f32[160,1]{0,1:T(1,128)}, u32[]{:S(2)}) copy-start(f32[160,1]{0,1:T(1,128)} %get-tuple-element.206) | copy-start | bytes 1924
  843.7 31.5 %copy-start.111 = (f32[160,1]{0,1:T(1,128)S(1)}, f32[160,1]{0,1:T(1,128)}, u32[]{:S(2)}) copy-start(f32[160,1]{0,1:T(1,128)} %get-tuple-element.207) | copy-start | bytes 1924
  898.0 35.0 %copy-start.21 = (f32[160,4096]{1,0:T(8,128)S(1)}, f32[160,4096]{1,0:T(8,128)}, u32[]{:S(2)}) copy-start(f32[160,4096]{1,0:T(8,128)} %param.24) | copy-start | bytes 7864324
  898.0 35.0 %copy-start.69 = (f32[160,8]{0,1:T(8,128)S(1)}, f32[160,8]{0,1:T(8,128)}, u32[]{:S(2)}) copy-start(f32[160,8]{0,1:T(8,128)} %stack.25) | copy-start | bytes 15364
  (73 other events, 169.3 us)
Sparse Core Ops, SparseCore 0:
  10.2 46.2 all-gather.6
  63.5 26.7 all-gather.8
  92.4 31.8 all-gather.10
  126.4 97.1 all-gather.12
  225.5 53.0 all-gather.14
  319.4 26.0 reduce-scatter.5
  348.3 29.8 reduce-scatter.9
  381.1 50.8 reduce-scatter.13
  434.9 41.1 reduce-scatter.7
  478.3 92.8 reduce-scatter.11
  879.6 51.8 all-reduce.14
where the time goes:
time: 953 us; the launch traced here: 946 us
  waiting for transfers between devices  406 us (43%)
  other arithmetic  282 us (30%)
  matrix products  110 us (12%)
  blocking collectives  73.2 us (8%)
  between operations  38.5 us (4%)
  local copies, waits for them, and re-layouts  35.1 us (4%)
    reduce_sum x40, other arithmetic, orthonormal(): vector = vector - jnp.sum(basis * vector) * basis  118 us
    all_gather x1, waiting for transfers between devices, on_device(): lax.all_gather(master_expand.astype(jnp.bfloat16), 'blk', axis=0, tiled=T...  95.7 us
    reduce_scatter x1, waiting for transfers between devices, on_device(): lax.psum_scatter(grad_expand.astype(jnp.bfloat16), 'blk', scatter_dimensi...  90.7 us
    mul x4, other arithmetic, orthonormal(): columns.append(vector * lax.rsqrt(jnp.sum(vector * vector) + NORM_EPS))  72.7 us
    all_gather x1, waiting for transfers between devices, on_device(): lax.all_gather(master_reduce.astype(jnp.bfloat16), 'blk', axis=0, tiled=T...  43.6 us
    reduce_scatter x1, waiting for transfers between devices, on_device(): lax.psum_scatter(grad_attend.astype(jnp.bfloat16), 'blk', scatter_dimensi...  39 us
    reduce_scatter x1, waiting for transfers between devices, on_device(): lax.psum_scatter(grad_reduce.astype(jnp.bfloat16), 'blk', scatter_dimensi...  35.1 us
    reduce_sum x20, other arithmetic, orthonormal(): columns.append(vector * lax.rsqrt(jnp.sum(vector * vector) + NORM_EPS))  30.8 us
  transfers between devices with their start and end apart: 11, of which 10 were waited for; matrix products, arithmetic and copies ran while one was open for 12% of the time, Pallas kernels for 0%

commit v1 on v0

--- a/solution.py
+++ b/solution.py
@@ -273,7 +273,7 @@
     right_sums = (
         lax.psum(rights[0].astype(jnp.bfloat16), "grp").astype(jnp.float32),
         lax.psum(rights[1].astype(jnp.bfloat16), "grp").astype(jnp.float32),
-        lax.psum(rights[2].astype(jnp.bfloat16), "grp").astype(jnp.float32),
+        jnp.sum(lax.all_gather(rights[2].astype(jnp.bfloat16), "grp"), axis=0).astype(jnp.float32),
         lax.psum(rights[3].astype(jnp.bfloat16), "grp").astype(jnp.float32),
     )
     residues = [

time: 953 us -> 935 us (0.981)
  waiting for transfers between devices: 406 us -> 377 us
  blocking collectives: 73.2 us -> 83.7 us
    psum x1 -> x0, waiting for transfers between devices: 29.5 us -> none  [on_device(): lax.psum(rights[2].astype(jnp.bfloat16), 'grp').astype(jnp.float32)]
    all_gather x0 -> x1, blocking collectives: none -> 9.91 us  [on_device(): lax.all_gather(rights[2].astype(jnp.bfloat16), 'grp')]
    unnamed x261 -> x243, local copies, waits for them, and re-layouts: 20 us -> 19.9 us
  transfers between devices with their start and end apart: 11 -> 10, of which waited for: 10 -> 9; matrix products, arithmetic and copies ran while one was open for 12% -> 10% of each run, Pallas kernels for 0% -> 0%
where the time goes in v1:
time: 935 us; the launch traced here: 927 us
  waiting for transfers between devices  377 us (40%)
  other arithmetic  283 us (30%)
  matrix products  108 us (12%)
  blocking collectives  83.7 us (9%)
  between operations  38.7 us (4%)
  local copies, waits for them, and re-layouts  36.6 us (4%)
    reduce_sum x40, other arithmetic, orthonormal(): vector = vector - jnp.sum(basis * vector) * basis  118 us
    all_gather x1, waiting for transfers between devices, on_device(): lax.all_gather(master_expand.astype(jnp.bfloat16), 'blk', axis=0, tiled=T...  95.7 us
    reduce_scatter x1, waiting for transfers between devices, on_device(): lax.psum_scatter(grad_expand.astype(jnp.bfloat16), 'blk', scatter_dimensi...  90.7 us
    mul x4, other arithmetic, orthonormal(): columns.append(vector * lax.rsqrt(jnp.sum(vector * vector) + NORM_EPS))  73.3 us
    all_gather x1, waiting for transfers between devices, on_device(): lax.all_gather(master_reduce.astype(jnp.bfloat16), 'blk', axis=0, tiled=T...  43.6 us
    reduce_scatter x1, waiting for transfers between devices, on_device(): lax.psum_scatter(grad_attend.astype(jnp.bfloat16), 'blk', scatter_dimensi...  39 us
    reduce_scatter x1, waiting for transfers between devices, on_device(): lax.psum_scatter(grad_reduce.astype(jnp.bfloat16), 'blk', scatter_dimensi...  35.1 us
    reduce_sum x20, other arithmetic, orthonormal(): columns.append(vector * lax.rsqrt(jnp.sum(vector * vector) + NORM_EPS))  30.7 us
  transfers between devices with their start and end apart: 10, of which 9 were waited for; matrix products, arithmetic and copies ran while one was open for 10% of the time, Pallas kernels for 0%

profile of v1, /device:TPU:0, one launch (start us, length us, event | category | flops | bytes accessed | tf_op | source)
XLA Modules:
  0.0 927.2 jit_solution(7239983367907526645)
XLA Ops:
  10.2 14.9 %all-gather.1 = bf16[4,1,768]{2,1,0:T(2,128)(2,1)S(1)} all-gather(bf16[1,1,768]{2,1,0:T(2,128)(2,1)S(1)} %reshape.432), channel_id=1, replica_groups=mesh['grp'=8,'blk'=4] {'blk'}, dimensions={0}, use_global_device_ids=true | all-gather | bytes 7680 | tf_op jit(solution)/shard_map/all_gather | solution.py:112
  27.0 29.5 %all-gather.8.cloned.1.call-done = bf16[640,1536]{1,0:T(8,128)(2,1)} async-done(((bf16[160,1536]{1,0:T(8,128)(2,1)}), bf16[640,1536]{1,0:T(8,128)(2,1)}) %all-gather.8.cloned.1.call-update) | async-done | bytes 1966096 | tf_op jit(solution)/shard_map/all_gather | solution.py:108
  56.5 2.9 fusion.142
  69.1 2.8 fusion.83
  83.9 6.4 all-gather.10.cloned.1.call-done
  98.5 25.9 %all-gather.12.cloned.1.call-done = bf16[1024,640]{1,0:T(8,128)(2,1)} async-done(((bf16[256,640]{1,0:T(8,128)(2,1)}), bf16[1024,640]{1,0:T(8,128)(2,1)}) %all-gather.12.cloned.1.call-update) | async-done | bytes 1310736 | tf_op jit(solution)/shard_map/all_gather | solution.py:109
  127.8 95.7 %all-gather.14.cloned.1.call-done = bf16[640,4096]{1,0:T(8,128)(2,1)} async-done(((bf16[160,4096]{1,0:T(8,128)(2,1)}), bf16[640,4096]{1,0:T(8,128)(2,1)}) %all-gather.14.cloned.1.call-update) | async-done | bytes 5242896 | tf_op jit(solution)/shard_map/all_gather | solution.py:110
  223.5 5.5 fusion.123
  229.0 3.3 copy-done.4
  232.4 2.6 multiply_convert_fusion
  235.0 43.6 %all-gather.16.cloned.1.call-done = bf16[2048,640]{1,0:T(8,128)(2,1)} async-done(((bf16[512,640]{1,0:T(8,128)(2,1)}), bf16[2048,640]{1,0:T(8,128)(2,1)}) %all-gather.16.cloned.1.call-update) | async-done | bytes 2621456 | tf_op jit(solution)/shard_map/all_gather | solution.py:111
  278.6 4.4 multiply_reduce_fusion.6
  285.5 4.9 fusion.34
  290.6 4.1 multiply_reduce_fusion.2
  300.5 2.9 copy.142
  303.5 5.3 fusion
  310.3 3.2 fusion.2
  313.5 3.1 convolution_bitcast_fusion.2
  319.3 3.6 convolution_convert_fusion.3
  323.0 4.4 convolution_convert_fusion.1
  328.8 3.2 convolution_bitcast_fusion
  334.8 10.6 %reduce-scatter.6.cloned.1.call-done = bf16[256,512]{1,0:T(8,128)(2,1)} async-done(((bf16[1024,512]{1,0:T(8,128)(2,1)}), bf16[256,512]{1,0:T(8,128)(2,1)}) %reduce-scatter.6.cloned.1.call-update) | async-done | bytes 262160 | tf_op jit(solution)/shard_map/reduce_scatter | solution.py:221
  346.5 3.0 fusion.76
  349.7 3.6 multiply_reduce_fusion.9
  363.3 8.8 convolution_convert_fusion
  374.2 4.8 fusion.46
  380.2 9.7 %all-reduce.10 = bf16[3072]{0:T(1024)(128)(2,1)S(1)} all-reduce(bf16[3072]{0:T(1024)(128)(2,1)S(1)} %dynamic-update-slice.5), channel_id=8, replica_groups=mesh['grp'=8,'blk'=4] {'blk'}, use_global_device_ids=true, to_apply=%region_26.27.clone | all-reduce | flops 3072 | bytes 12288
  390.6 2.8 fusion.41
  396.9 35.1 %reduce-scatter.14.cloned.1.call-done = bf16[512,640]{1,0:T(8,128)(2,1)} async-done(((bf16[2048,640]{1,0:T(8,128)(2,1)}), bf16[512,640]{1,0:T(8,128)(2,1)}) %reduce-scatter.14.cloned.1.call-update) | async-done | bytes 655376 | tf_op jit(solution)/shard_map/reduce_scatter | solution.py:252
  434.3 2.8 fusion.85
  437.1 39.0 %reduce-scatter.8.cloned.1.call-done = bf16[160,1536]{1,0:T(8,128)(2,1)} async-done(((bf16[640,1536]{1,0:T(8,128)(2,1)}), bf16[160,1536]{1,0:T(8,128)(2,1)}) %reduce-scatter.8.cloned.1.call-update) | async-done | bytes 491536 | tf_op jit(solution)/shard_map/reduce_scatter | solution.py:243
  480.5 90.7 %reduce-scatter.12.cloned.1.call-done = bf16[160,4096]{1,0:T(8,128)(2,1)} async-done(((bf16[640,4096]{1,0:T(8,128)(2,1)}), bf16[160,4096]{1,0:T(8,128)(2,1)}) %reduce-scatter.12.cloned.1.call-update) | async-done | bytes 1310736 | tf_op jit(solution)/shard_map/reduce_scatter | solution.py:249
  571.2 3.5 fusion.66
  574.7 25.0 %all-reduce.11 = (f32[160,8]{0,1:T(8,128)S(1)}, f32[256,8]{0,1:T(8,128)S(1)}, f32[160,8]{0,1:T(8,128)S(1)}, f32[512,8]{0,1:T(8,128)S(1)}, f32[768]{0:T(1024)}) all-reduce(f32[160,8]{0,1:T(8,128)S(1)} %fusion.88, f32[256,8]{0,1:T(8,128)S(1)} %fusion.92, f32[160,8]{0,1:T(8,128)S(1)} %fusion.66, ...), channel_id=1, replica_groups=mesh['grp'=8,'blk'=4] {'grp'}, use_global_device_ids=true, to_apply=%region_27.28 | all-reduce | flops 9472 | bytes 75776 | tf_op jit(solution)/shard_map/psum | solution.py:267
  603.6 5.1 multiply_reduce_fusion.126
  613.2 6.4 multiply_reduce_fusion.125
  620.3 3.8 multiply_reduce_fusion.124
  628.7 3.8 multiply_reduce_fusion.123
  633.2 2.5 multiply_reduce_fusion.122
  642.2 18.1 %subtract_multiply_fusion.21 = (f32[160,1]{0,1:T(1,128)S(1)}, f32[160,1]{0,1:T(1,128)S(1)}, f32[160,1]{0,1:T(1,128)S(1)}, f32[160,1]{0,1:T(1,128)S(1)}, f32[160,...) fusion(f32[160,1]{0,1:T(1,128)S(1)} %get-tuple-element.344, f32[]{:T(128)S(6)} %rsqrt.180, ...), kind=kLoop, calls=%fused_computation.453 | loop fusion | flops 10080 | bytes 9740 | tf_op jit(solution)/shard_map/mul | solution.py:65
  664.2 5.1 multiply_reduce_fusion.90
  673.9 6.4 multiply_reduce_fusion.89
  681.0 3.8 multiply_reduce_fusion.88
  689.3 3.8 multiply_reduce_fusion.87
  693.9 2.6 multiply_reduce_fusion.86
  702.8 18.6 %subtract_multiply_fusion.14 = (f32[256,1]{0,1:T(1,128)S(1)}, f32[256,1]{0,1:T(1,128)S(1)}, f32[256,1]{0,1:T(1,128)S(1)}, f32[256,1]{0,1:T(1,128)S(1)}, f32[256,...) fusion(f32[256,1]{0,1:T(1,128)S(1)} %get-tuple-element.336, f32[]{:T(128)S(6)} %rsqrt.188, ...), kind=kLoop, calls=%fused_computation.383 | loop fusion | flops 16128 | bytes 15500 | tf_op jit(solution)/shard_map/mul | solution.py:65
  725.3 5.1 multiply_reduce_fusion.54
  734.9 6.4 multiply_reduce_fusion.53
  742.0 3.9 multiply_reduce_fusion.52
  750.4 3.8 multiply_reduce_fusion.51
  763.8 18.5 %subtract_multiply_fusion.7 = (f32[160,1]{0,1:T(1,128)}, f32[160,1]{0,1:T(1,128)}, f32[160,1]{0,1:T(1,128)}, f32[160,1]{0,1:T(1,128)}, f32[160,1]{0,1:T(1,128)}, /*index=5*/f32[160,1]{0,1:T(1,128)}, f32[160,1]{0,1:T(1,128)}) fusion(f32[160,1]{0,1:T(1,128)S(1)} %get-tuple-element.328, f32[]{:T(128)S(6)} %rsqrt.196, f32[]{:T(128)} %get-tuple-element.208, ...), kind=kLoop, calls=%fused_computation.313 | loop fusion | flops 10080 | bytes 9740 | tf_op jit(solution)/shard_map/mul | solution.py:65
  786.2 5.1 multiply_reduce_fusion.18
  795.8 6.5 multiply_reduce_fusion.17
  802.9 3.9 multiply_reduce_fusion.16
  811.3 3.8 multiply_reduce_fusion.15
  821.5 2.6 multiply_reduce_fusion.13
  826.0 18.0 %subtract_multiply_fusion = (f32[512,1]{0,1:T(1,128)S(1)}, f32[512,1]{0,1:T(1,128)S(1)}, f32[512,1]{0,1:T(1,128)S(1)}, f32[512,1]{0,1:T(1,128)S(1)}, f32[512,1]{...) fusion(f32[512,1]{0,1:T(1,128)S(1)} %get-tuple-element.314, f32[]{:T(128)S(6)} %rsqrt.204, ...), kind=kLoop, calls=%fused_computation.222 | loop fusion | flops 32256 | bytes 30860 | tf_op jit(solution)/shard_map/mul | solution.py:65
  850.8 24.2 %all-reduce.12 = (bf16[1536,8]{0,1:T(8,128)(2,1)S(1)}, bf16[640,8]{0,1:T(8,128)(2,1)S(1)}, bf16[640,8]{0,1:T(8,128)(2,1)}) all-reduce(bf16[1536,8]{0,1:T(8,128)(2,1)S(1)} %get-tuple-element.361, bf16[640,8]{0,1:T(8,128)(2,1)} %get-tuple-element.363, bf16[640,8]{0,1:T(8,128)(2,1)} %get-tuple-element.365), channel_id=1, replica_groups=mesh['grp'=8,'blk'=4] {'grp'}, use_global_device_ids=true, to_apply=%region_175.176 | all-reduce | flops 22528 | bytes 90112 | tf_op jit(solution)/shard_map/psum | solution.py:274
  877.6 3.7 fusion.141
  881.3 9.9 %all-gather = bf16[32768,8]{0,1:T(8,128)(2,1)} all-gather(bf16[4096,8]{0,1:T(8,128)(2,1)S(1)} %get-tuple-element.367), channel_id=2, replica_groups=mesh['grp'=8,'blk'=4] {'grp'}, dimensions={0}, use_global_device_ids=true | all-gather | bytes 589824 | tf_op jit(solution)/shard_map/all_gather | solution.py:276
  894.3 3.9 fusion.129
  900.3 4.7 fusion.127
  905.0 2.7 fusion.126
  913.8 4.0 fusion.4
  (420 shorter events, 165.4 us)
Async XLA Ops:
  7.2 564.0 %copy-start = (f32[1,4096,8]{1,2,0:T(8,128)S(1)}, f32[1,4096,8]{1,2,0:T(8,128)}, u32[]{:S(2)}) copy-start(f32[1,4096,8]{1,2,0:T(8,128)} %param.38) | copy-start | bytes 393220
  7.2 17.9 %copy-start.22 = (bf16[1,2,256,640]{3,2,1,0:T(8,128)(2,1)S(1)}, bf16[1,2,256,640]{3,2,1,0:T(8,128)(2,1)}, u32[]{:S(2)}) copy-start(bf16[1,2,256,640]{3,2,1,0:T(8,128)(2,1)} %param.20) | copy-start | bytes 1966084
  7.2 49.2 %all-gather.8.cloned.1.call-start = ((), (), s32[]{:S(2)}) async-start(), calls=%async_computation.5 | async-start | bytes 2457600 | tf_op jit(solution)/shard_map/all_gather | solution.py:108
  9.4 80.9 %all-gather.10.cloned.1.call-start = ((), (), s32[]{:S(2)}) async-start(), calls=%async_computation.6 | async-start | bytes 1310720 | tf_op jit(solution)/shard_map/all_gather | solution.py:133
  25.4 31.1 %copy-start.92 = (f32[512]{0:T(512)}, f32[512]{0:T(512)S(1)}, u32[]{:S(2)}) copy-start(f32[512]{0:T(512)S(1)} %rsqrt.166) | copy-start | bytes 6148
  25.4 31.1 %copy-start.105 = (f32[128]{0:T(128)}, f32[128]{0:T(128)S(1)}, u32[]{:S(2)}) copy-start(f32[128]{0:T(128)S(1)} %multiply_power_fusion) | copy-start | bytes 1540
  26.0 34.4 %copy-start.86 = (f32[256]{0:T(256)}, f32[256]{0:T(256)S(1)}, u32[]{:S(2)}) copy-start(f32[256]{0:T(256)S(1)} %get-tuple-element.325) | copy-start | bytes 3076
  26.6 29.9 %copy-start.83 = (f32[640]{0:T(1024)}, f32[640]{0:T(1024)S(1)}, u32[]{:S(2)}) copy-start(f32[640]{0:T(1024)S(1)} %get-tuple-element.324) | copy-start | bytes 7684
  26.6 100.8 %copy-start.75 = (f32[640]{0:T(1024)}, f32[640]{0:T(1024)S(1)}, u32[]{:S(2)}) copy-start(f32[640]{0:T(1024)S(1)} %get-tuple-element.323) | copy-start | bytes 7684
  26.7 33.6 %copy-start.42 = (f32[512,128]{1,0:T(8,128)}, f32[512,128]{1,0:T(8,128)S(1)}, u32[]{:S(2)}) copy-start(f32[512,128]{1,0:T(8,128)S(1)} %broadcast_multiply_fusion.1) | copy-start | bytes 786436
  27.0 32.4 %copy-start.56 = (bf16[512,640]{1,0:T(8,128)(2,1)}, bf16[512,640]{1,0:T(8,128)(2,1)S(1)}, u32[]{:S(2)}) copy-start(bf16[512,640]{1,0:T(8,128)(2,1)S(1)} %fusion.45) | copy-start | bytes 1966084
  59.9 5.5 copy-start.20
  63.3 61.0 %all-gather.12.cloned.1.call-start = ((), (), s32[]{:S(2)}) async-start(), calls=%async_computation.7 | async-start | bytes 1638400 | tf_op jit(solution)/shard_map/all_gather | solution.py:109
  65.3 158.3 %all-gather.14.cloned.1.call-start = ((), (), s32[]{:S(2)}) async-start(), calls=%async_computation.8 | async-start | bytes 6553600 | tf_op jit(solution)/shard_map/all_gather | solution.py:110
  66.6 212.1 %all-gather.16.cloned.1.call-start = ((), (), s32[]{:S(2)}) async-start(), calls=%async_computation.9 | async-start | bytes 3276800 | tf_op jit(solution)/shard_map/all_gather | solution.py:111
  68.8 276.7 %reduce-scatter.6.cloned.1.call-start = ((), (), s32[]{:S(2)}) async-start(), calls=%async_computation.10 | async-start | bytes 1310720 | tf_op jit(solution)/shard_map/reduce_scatter | solution.py:221
  72.6 21.8 %copy-start.26 = (pred[2,256,768]{1,2,0:T(8,128)(4,1)}, pred[2,256,768]{1,2,0:T(8,128)(4,1)S(1)}, u32[]{:S(2)}) copy-start(pred[2,256,768]{1,2,0:T(8,128)(4,1)S(1)} %fusion.31) | copy-start | bytes 1179652
  74.4 6.4 copy-start.2
  83.9 8.1 copy-start.44
  98.5 28.3 %copy-start.53 = (bf16[64,8,4,256]{3,1,2,0:T(8,128)(2,1)}, bf16[64,8,4,256]{3,1,2,0:T(8,128)(2,1)S(1)}, u32[]{:S(2)}) copy-start(bf16[64,8,4,256]{3,1,2,0:T(8,128)(2,1)S(1)} %copy.168) | copy-start | bytes 3145732
  235.0 48.0 %copy-start.34 = (bf16[1,2,256,640]{3,2,1,0:T(8,128)(2,1)S(1)}, bf16[1,2,256,640]{3,2,1,0:T(8,128)(2,1)}, u32[]{:S(2)}) copy-start(bf16[1,2,256,640]{3,2,1,0:T(8,128)(2,1)} %param.21) | copy-start | bytes 1966084
  235.0 48.0 %copy-start.85 = (f32[640]{0:T(1024)S(1)}, f32[640]{0:T(1024)}, u32[]{:S(2)}) copy-start(f32[640]{0:T(1024)} %get-tuple-element.321) | copy-start | bytes 7684
  278.6 6.9 copy-start.5
  284.2 6.4 slice-start.2
  285.5 5.0 copy-start.55
  285.5 5.0 slice-start.3
  290.5 4.1 copy-start.39
  290.5 4.1 copy-start.40
  290.6 4.1 copy-start.76
  300.5 8.3 slice-start
  303.4 5.3 slice-start.1
  303.4 5.3 copy-start.27
  303.4 5.3 copy-start.41
  303.5 5.3 copy-start.72
  310.3 7.0 copy-start.8
  319.2 74.2 %reduce-scatter.10.cloned.1.call-start = ((), (), s32[]{:S(2)}) async-start(), calls=%async_computation.12 | async-start | bytes 1638400 | tf_op jit(solution)/shard_map/reduce_scatter | solution.py:246
  322.9 109.1 %reduce-scatter.14.cloned.1.call-start = ((), (), s32[]{:S(2)}) async-start(), calls=%async_computation.14 | async-start | bytes 3276800 | tf_op jit(solution)/shard_map/reduce_scatter | solution.py:252
  327.5 148.7 %reduce-scatter.8.cloned.1.call-start = ((), (), s32[]{:S(2)}) async-start(), calls=%async_computation.11 | async-start | bytes 2457600 | tf_op jit(solution)/shard_map/reduce_scatter | solution.py:243
  345.4 4.2 copy-start.38
  345.4 4.2 copy-start.43
  345.5 4.2 copy-start.78
  345.5 4.2 copy-start.87
  353.3 6.6 copy-start.59
  363.2 208.0 %reduce-scatter.12.cloned.1.call-start = ((), (), s32[]{:S(2)}) async-start(), calls=%async_computation.13 | async-start | bytes 6553600 | tf_op jit(solution)/shard_map/reduce_scatter | solution.py:249
  374.1 5.1 copy-start.100
  374.1 5.3 copy-start.109
  374.1 5.5 copy-start.99
  374.1 5.7 copy-start.108
  374.1 5.9 copy-start.107
  374.1 16.5 %copy-start.97 = (f32[1,2,2,128]{3,1,2,0:T(2,128)S(1)}, f32[1,2,2,128]{3,1,2,0:T(2,128)}, u32[]{:S(2)}) copy-start(f32[1,2,2,128]{3,1,2,0:T(2,128)} %copy-done.96) | copy-start | bytes 6148
  374.1 16.5 %copy-start.19 = (f32[512,640]{1,0:T(8,128)S(1)}, f32[512,640]{1,0:T(8,128)}, u32[]{:S(2)}) copy-start(f32[512,640]{1,0:T(8,128)} %copy-done.18) | copy-start | bytes 3932164
  390.6 4.7 copy-start.32
  390.6 4.7 copy-start.91
  393.4 40.9 %copy-start.90 = (f32[1,640,8]{1,2,0:T(8,128)S(1)}, f32[1,640,8]{1,2,0:T(8,128)}, u32[]{:S(2)}) copy-start(f32[1,640,8]{1,2,0:T(8,128)} %param.39) | copy-start | bytes 61444
  396.9 79.2 %copy-start.79 = (f32[1,1536,8]{1,2,0:T(8,128)S(1)}, f32[1,1536,8]{1,2,0:T(8,128)}, u32[]{:S(2)}) copy-start(f32[1,1536,8]{1,2,0:T(8,128)} %param.36) | copy-start | bytes 147460
  434.3 136.9 %copy-start.6 = (f32[1,160,4096]{2,1,0:T(8,128)S(1)}, f32[1,160,4096]{2,1,0:T(8,128)}, u32[]{:S(2)}) copy-start(f32[1,160,4096]{2,1,0:T(8,128)} %param.34) | copy-start | bytes 7864324
  844.0 66.1 %copy-start.65 = (f32[160,8]{0,1:T(8,128)}, f32[160,8]{0,1:T(8,128)S(1)}, u32[]{:S(2)}) copy-start(f32[160,8]{0,1:T(8,128)S(1)} %stack.23) | copy-start | bytes 15364
  844.8 67.4 %copy-start.66 = (f32[256,8]{0,1:T(8,128)}, f32[256,8]{0,1:T(8,128)S(1)}, u32[]{:S(2)}) copy-start(f32[256,8]{0,1:T(8,128)S(1)} %stack.24) | copy-start | bytes 24580
  844.8 73.0 %copy-start.64 = (f32[512,8]{0,1:T(8,128)}, f32[512,8]{0,1:T(8,128)S(1)}, u32[]{:S(2)}) copy-start(f32[512,8]{0,1:T(8,128)S(1)} %stack.26) | copy-start | bytes 49156
  844.8 4.5 copy-start.16
  894.3 5.7 copy-start.45
  900.3 4.7 copy-start.37
  900.3 4.7 copy-start.52
  900.3 4.7 copy-start.80
  (63 other events, 134.5 us)
Sparse Core Ops, SparseCore 0:
  10.2 46.2 all-gather.7
  63.5 26.7 all-gather.9
  92.4 31.8 all-gather.11
  126.4 97.1 all-gather.13
  225.5 53.0 all-gather.15
  319.4 26.0 reduce-scatter.5
  348.3 29.8 reduce-scatter.9
  381.1 50.8 reduce-scatter.13
  434.9 41.1 reduce-scatter.7
  478.3 92.8 reduce-scatter.11
